TPU v7x, 32 devices: a whole 2x2x4 slice. The times are simulated.
32 devices in a mesh: row: 4 (over z), col: 8 (over y, x, core).
Axes of the slice: x: 2, y: 2, z: 4, core: 2. Of those that a mesh axis runs over, the one named last changes fastest.
Arguments:
- weight: float32 [16384, 16384], P('row', 'col'), may hold values from -0.046875 to 0.046875
- leak: float32 [16384], P('col'), may hold values from 0.1 to 1
- rates: float32 [3, 256, 16384], P(None, 'row', 'col'), may hold values from -0.95 to 0.95
- cotangent: float32 [256, 16384], P('row', 'col'), may hold values from -2 to 2
Outputs:
- grad_input: float32 [256, 16384], P('row', 'col')
- grad_weight: float32 [16384, 16384], P('row', 'col')
- grad_noise: float32 [3, 16384], P(None, 'row')
All inputs are finite; a program needn't handle non-finite values.
Results may differ from a plain program's by a relative error of at most 0.0001.
Values sent between devices are 32-bit elements; how exact they have to be, the bound alone decides.
A program may use at most 192 MiB of HBM per device.

v0:
```python
import jax
import jax.numpy as jnp
from jax import lax
from jax.sharding import PartitionSpec as P

TSTEPS = 3


def shards(weight, leak, rates, cotangent):
    n_col = lax.axis_size("col")
    own_rows = cotangent.shape[0]
    local_units = cotangent.shape[1]
    full_rates = lax.all_gather(rates, "row", axis=1, tiled=True)
    grad_weight = jnp.zeros(weight.shape, jnp.float32)
    noise_list = []
    carried = cotangent
    for step_back in range(TSTEPS - 1, -1, -1):
        scaled = leak[None, :] * carried
        spread = scaled.reshape(own_rows, local_units // n_col, n_col)
        by_col = lax.all_to_all(spread, "col", split_axis=2, concat_axis=1, tiled=True)
        by_row = lax.all_to_all(by_col, "row", split_axis=1, concat_axis=0, tiled=True)
        gathered = lax.all_gather(by_row, "col", axis=2, tiled=True)
        unit_block = gathered.reshape(gathered.shape[0], gathered.shape[1] * gathered.shape[2])
        rates_now = full_rates[step_back]
        noise_list.insert(0, jnp.sum(unit_block, axis=0))
        grad_weight = grad_weight + lax.dot_general(
            unit_block,
            rates_now,
            (((0,), (0,)), ((), ())),
            precision=lax.Precision.HIGHEST,
            preferred_element_type=jnp.float32,
        )
        partial_sum = jnp.dot(
            unit_block, weight, precision=lax.Precision.HIGHEST, preferred_element_type=jnp.float32
        )
        adjoint = lax.psum_scatter(partial_sum, "row", scatter_dimension=0, tiled=True)
        local_rates = rates[step_back]
        carried = (1.0 - leak[None, :]) * carried + (1.0 - local_rates * local_rates) * adjoint
    return (carried, grad_weight, jnp.stack(noise_list))


def solution(mesh):
    placed = (P("row", "col"), P("col"), P(None, "row", "col"), P("row", "col"))
    return jax.shard_map(
        shards,
        mesh=mesh,
        in_specs=placed,
        out_specs=(P("row", "col"), P("row", "col"), P(None, "row")),
        check_vma=False,
    )
```

profile of v0, /device:TPU:0, one launch (start us, length us, event | category | flops | bytes accessed | tf_op | source)
XLA Modules:
  0.0 634.5 jit_solution(5892808969612367369)
XLA Ops:
  7.2 1.1 broadcast_multiply_fusion.2
  8.3 0.3 copy.19
  8.6 0.4 copy.20
  9.0 14.7 %all_to_all.108 = f32[64,256,8]{1,0,2:T(8,128)S(1)} all-to-all(f32[64,256,8]{1,0,2:T(8,128)S(1)} %copy.20), channel_id=1, replica_groups=mesh['row'=4,'col'=8] {'col'}, dimensions={2} | all-to-all | bytes 1048576 | tf_op jit(solution)/shard_map/all_to_all | solution.py:20
  23.7 0.3 copy.43
  24.1 0.5 broadcast.24
  24.6 9.3 %reduce.3 = f32[2048,64]{1,0:T(8,128)S(1)} reduce(f32[2048,1,64]{2,1,0:T(1,128)S(1)} %bitcast.75, f32[]{:T(128)} %broadcast.24), dimensions={1}, to_apply=%bitcast.64.reduce_sub_computation | reduce | bytes 1048580
  33.9 0.7 reshape.48
  34.6 18.6 %all_to_all.109 = f32[4,1,32768]{2,1,0:T(1,128)S(1)} all-to-all(f32[4,1,32768]{2,1,0:T(1,128)S(1)} %reshape.48), channel_id=1, replica_groups=mesh['row'=4,'col'=8] {'row'}, dimensions={0} | all-to-all | bytes 1048576 | tf_op jit(solution)/shard_map/all_to_all | solution.py:21
  53.2 2.1 reduce.4
  55.3 1.3 reshape.49
  56.6 0.4 copy.44
  57.0 1.0 copy.24
  58.0 0.3 reduce-scatter.4.cloned.1.call-start
  58.3 34.2 %all-gather.5.cloned.1.call-done = f32[256,512,8]{1,0,2:T(8,128)} async-done(((f32[256,512,1]{1,0,2:T(8,128)}), f32[256,512,8]{1,0,2:T(8,128)}) %all-gather.5.cloned.1.call-update) | async-done | bytes 4194320 | tf_op jit(solution)/shard_map/all_gather | solution.py:22
  92.6 5.4 copy.25
  98.0 33.9 %fusion.9 = f32[256,2048]{1,0:T(8,128)} fusion(f32[4096,2048]{1,0:T(8,128)} %param.4, f32[256,512,8]{0,2,1:T(8,128)} %copy.25), kind=kOutput, calls=%fused_computation.10 | convolution fusion | flops 25769803776 | bytes 39845888 | tf_op jit(solution)/shard_map/dot_general | solution.py:33
  132.0 43.7 %reduce-scatter.4.cloned.1.call-done = f32[64,2048]{1,0:T(8,128)} async-done(((f32[256,2048]{1,0:T(8,128)}), f32[64,2048]{1,0:T(8,128)}) %reduce-scatter.4.cloned.1.call-update) | async-done | bytes 524304 | tf_op jit(solution)/shard_map/reduce_scatter | solution.py:36
  175.7 1.3 broadcast_multiply_fusion.1
  177.0 0.3 copy.26
  177.3 0.4 copy.27
  177.7 13.7 %all_to_all.110 = f32[64,256,8]{1,0,2:T(8,128)S(1)} all-to-all(f32[64,256,8]{1,0,2:T(8,128)S(1)} %copy.27), channel_id=1, replica_groups=mesh['row'=4,'col'=8] {'col'}, dimensions={2} | all-to-all | bytes 1048576 | tf_op jit(solution)/shard_map/all_to_all | solution.py:20
  191.4 0.3 copy.45
  191.8 9.3 %reduce.5 = f32[2048,64]{1,0:T(8,128)S(1)} reduce(f32[2048,1,64]{2,1,0:T(1,128)S(1)} %bitcast.76, f32[]{:T(128)} %broadcast.24), dimensions={1}, to_apply=%bitcast.66.reduce_sub_computation | reduce | bytes 1048580
  201.1 0.7 reshape.50
  201.8 16.6 %all_to_all.111 = f32[4,1,32768]{2,1,0:T(1,128)S(1)} all-to-all(f32[4,1,32768]{2,1,0:T(1,128)S(1)} %reshape.50), channel_id=1, replica_groups=mesh['row'=4,'col'=8] {'row'}, dimensions={0} | all-to-all | bytes 1048576 | tf_op jit(solution)/shard_map/all_to_all | solution.py:21
  218.4 2.1 reduce.6
  220.5 1.3 reshape.51
  221.8 0.4 copy.46
  222.2 1.0 copy.31
  223.2 0.2 reduce-scatter.6.cloned.1.call-start
  223.4 34.3 %all-gather.7.cloned.1.call-done = f32[256,512,8]{1,0,2:T(8,128)} async-done(((f32[256,512,1]{1,0,2:T(8,128)}), f32[256,512,8]{1,0,2:T(8,128)}) %all-gather.7.cloned.1.call-update) | async-done | bytes 4194320 | tf_op jit(solution)/shard_map/all_gather | solution.py:22
  257.7 5.5 copy.32
  263.2 33.8 %fusion.5 = f32[256,2048]{1,0:T(8,128)} fusion(f32[4096,2048]{1,0:T(8,128)} %param.4, f32[256,512,8]{0,2,1:T(8,128)} %copy.32), kind=kOutput, calls=%fused_computation.6 | convolution fusion | flops 25769803776 | bytes 39845888 | tf_op jit(solution)/shard_map/dot_general | solution.py:33
  297.2 0.5 all-gather.11.cloned.1.call-update
  297.8 43.2 %reduce-scatter.6.cloned.1.call-done = f32[64,2048]{1,0:T(8,128)} async-done(((f32[256,2048]{1,0:T(8,128)}), f32[64,2048]{1,0:T(8,128)}) %reduce-scatter.6.cloned.1.call-update) | async-done | bytes 524304 | tf_op jit(solution)/shard_map/reduce_scatter | solution.py:36
  340.9 2.0 broadcast_multiply_fusion
  343.0 0.3 copy.33
  343.3 0.4 copy.34
  343.7 13.5 %all_to_all.112 = f32[64,256,8]{1,0,2:T(8,128)} all-to-all(f32[64,256,8]{1,0,2:T(8,128)S(1)} %copy.34), channel_id=1, replica_groups=mesh['row'=4,'col'=8] {'col'}, dimensions={2} | all-to-all | bytes 1048576 | tf_op jit(solution)/shard_map/all_to_all | solution.py:20
  357.2 1.4 copy.47
  358.5 10.3 %reduce.7 = f32[2048,64]{1,0:T(8,128)} reduce(f32[2048,1,64]{2,1,0:T(1,128)S(1)} %bitcast.77, f32[]{:T(128)} %broadcast.24), dimensions={1}, to_apply=%bitcast.68.reduce_sub_computation | reduce | bytes 1048580
  368.9 1.9 reshape.52
  370.7 32.0 %all_to_all.113 = f32[4,1,32768]{2,1,0:T(1,128)S(1)} all-to-all(f32[4,1,32768]{2,1,0:T(1,128)S(1)} %reshape.52), channel_id=1, replica_groups=mesh['row'=4,'col'=8] {'row'}, dimensions={0} | all-to-all | bytes 1048576 | tf_op jit(solution)/shard_map/all_to_all | solution.py:21
  402.7 2.1 reduce.8
  404.8 1.3 reshape.53
  406.1 0.4 copy.48
  406.5 1.0 copy.38
  407.5 0.3 reduce-scatter.8.cloned.1.call-start
  407.8 2.6 reduce_sum.29
  410.4 0.1 copy.42
  410.6 0.2 stack.14
  410.7 57.2 %all-gather.11.cloned.1.call-done = f32[3,256,2048]{2,1,0:T(8,128)} async-done(((f32[3,64,2048]{2,1,0:T(8,128)}), f32[3,256,2048]{2,1,0:T(8,128)}) %all-gather.11.cloned.1.call-update) | async-done | bytes 6291472 | tf_op jit(solution)/shard_map/all_gather | solution.py:13
  468.0 32.4 %fusion.7 = f32[4096,2048]{1,0:T(8,128)} fusion(f32[256,512,8]{0,2,1:T(8,128)} %copy.25, f32[3,256,2048]{2,1,0:T(8,128)} %all-gather.11.cloned.1.call-done), kind=kOutput, calls=%fused_computation.8 | convolution fusion | flops 25769803776 | bytes 39845888 | tf_op jit(solution)/shard_map/dot_general | solution.py:26
  500.4 2.7 reduce_sum.28
  503.2 0.2 stack.13
  503.4 32.7 %fusion.3 = f32[4096,2048]{1,0:T(8,128)} fusion(f32[256,512,8]{0,2,1:T(8,128)} %copy.32, f32[3,256,2048]{2,1,0:T(8,128)} %all-gather.11.cloned.1.call-done), kind=kOutput, calls=%fused_computation.4 | convolution fusion | flops 25769803776 | bytes 39845888 | tf_op jit(solution)/shard_map/dot_general | solution.py:26
  536.0 2.6 reduce_sum.27
  538.8 0.2 stack.12
  539.0 5.5 copy.39
  544.4 33.9 %fusion.1 = f32[256,2048]{1,0:T(8,128)} fusion(f32[4096,2048]{1,0:T(8,128)} %param.4, f32[256,512,8]{0,2,1:T(8,128)} %copy.39), kind=kOutput, calls=%fused_computation.2 | convolution fusion | flops 25769803776 | bytes 39845888 | tf_op jit(solution)/shard_map/dot_general | solution.py:33
  578.4 0.7 pad_maximum_fusion
  579.1 46.4 %add_add_fusion = f32[4096,2048]{1,0:T(8,128)} fusion(f32[4096,2048]{1,0:T(8,128)} %fusion.7, f32[4096,2048]{1,0:T(8,128)} %fusion.3, f32[256,512,8]{0,2,1:T(8,128)} %copy.39, f32[3,256,2048]{2,1,0:T(8,128)} %all-gather.11.cloned.1.call-done), kind=kOutput, calls=%fused_computation | convolution fusion | flops 25786580992 | bytes 106954752 | tf_op jit(solution)/shard_map/dot_general | solution.py:26
  625.4 1.9 fusion.11
  (25 shorter events, 0.5 us)
Async XLA Ops:
  7.2 85.4 %all-gather.5.cloned.1.call-start = ((), (), s32[]{:S(2)}) async-start(), calls=%async_computation.9 | async-start | bytes 4718592 | tf_op jit(solution)/shard_map/all_gather | solution.py:22
  58.0 117.7 %reduce-scatter.4.cloned.1.call-start = ((), (), s32[]{:S(2)}) async-start(), calls=%async_computation.10 | async-start | bytes 2621440 | tf_op jit(solution)/shard_map/reduce_scatter | solution.py:36
  98.0 33.9 %copy-start.4 = (f32[2048]{0:T(1024)S(1)}, f32[2048]{0:T(1024)}, u32[]{:S(2)}) copy-start(f32[2048]{0:T(1024)} %param.5) | copy-start | bytes 24580
  98.0 77.7 %copy-start.1 = (f32[64,2048]{1,0:T(8,128)S(1)}, f32[64,2048]{1,0:T(8,128)}, u32[]{:S(2)}) copy-start(f32[64,2048]{1,0:T(8,128)} %param.7) | copy-start | bytes 1572868
  131.9 125.9 %all-gather.7.cloned.1.call-start = ((), (), s32[]{:S(2)}) async-start(), calls=%async_computation.11 | async-start | bytes 4718592 | tf_op jit(solution)/shard_map/all_gather | solution.py:22
  223.2 117.7 %reduce-scatter.6.cloned.1.call-start = ((), (), s32[]{:S(2)}) async-start(), calls=%async_computation.12 | async-start | bytes 2621440 | tf_op jit(solution)/shard_map/reduce_scatter | solution.py:36
  263.2 77.7 %copy-start.3 = (f32[64,2048]{1,0:T(8,128)S(1)}, f32[64,2048]{1,0:T(8,128)}, u32[]{:S(2)}) copy-start(f32[64,2048]{1,0:T(8,128)} %reduce-scatter.4.cloned.1.call-done) | copy-start | bytes 1572868
  297.1 43.8 %copy-start = (f32[3,64,2048]{2,1,0:T(8,128)S(1)}, f32[3,64,2048]{2,1,0:T(8,128)}, u32[]{:S(2)}) copy-start(f32[3,64,2048]{2,1,0:T(8,128)} %param.6) | copy-start | bytes 4718596
  297.1 170.9 %all-gather.11.cloned.1.call-start = ((), (), s32[]{:S(2)}) async-start(), calls=%async_computation.15 | async-start | bytes 7864320 | tf_op jit(solution)/shard_map/all_gather | solution.py:13
  297.7 238.3 %all-gather.9.cloned.1.call-start = ((), (), s32[]{:S(2)}) async-start(), calls=%async_computation.13 | async-start | bytes 4718592 | tf_op jit(solution)/shard_map/all_gather | solution.py:22
  407.5 217.9 %reduce-scatter.8.cloned.1.call-start = ((), (), s32[]{:S(2)}) async-start(), calls=%async_computation.14 | async-start | bytes 2621440 | tf_op jit(solution)/shard_map/reduce_scatter | solution.py:36
  579.1 46.4 %copy-start.2 = (f32[64,2048]{1,0:T(8,128)S(1)}, f32[64,2048]{1,0:T(8,128)}, u32[]{:S(2)}) copy-start(f32[64,2048]{1,0:T(8,128)} %get-tuple-element.4) | copy-start | bytes 1572868
Sparse Core Ops, SparseCore 0:
  58.1 34.4 all-gather.4
  132.0 43.6 reduce-scatter.3
  223.3 34.4 all-gather.6
  297.2 43.6 reduce-scatter.5
  342.3 125.6 all-gather.10
  469.7 34.7 all-gather.8
  578.5 41.7 reduce-scatter.7
where the time goes:
time: 642 us; the launch traced here: 634 us
  waiting for transfers between devices  213 us (33%)
  matrix products  213 us (33%)
  blocking collectives  109 us (17%)
  other arithmetic  50.4 us (8%)
  local copies, waits for them, and re-layouts  33 us (5%)
  between operations  14.6 us (2%)
    dot_general x3, matrix products, shards(): lax.dot_general(unit_block, rates_now, (((0,), (0,)), ((), ())), precisio...  111 us
    dot_general x3, matrix products, shards(): jnp.dot(unit_block, weight, precision=lax.Precision.HIGHEST, preferred_el...  102 us
    reduce_scatter x3, waiting for transfers between devices, shards(): lax.psum_scatter(partial_sum, 'row', scatter_dimension=0, tiled=True)  86.9 us
    all_gather x3, waiting for transfers between devices, shards(): gathered = lax.all_gather(by_row, 'col', axis=2, tiled=True)  68.6 us
    all_to_all x3, blocking collectives, shards(): lax.all_to_all(by_col, 'row', split_axis=1, concat_axis=0, tiled=True)  67.2 us
    all_gather x1, waiting for transfers between devices, shards(): full_rates = lax.all_gather(rates, 'row', axis=1, tiled=True)  57.2 us
    all_to_all x3, blocking collectives, shards(): lax.all_to_all(spread, 'col', split_axis=2, concat_axis=1, tiled=True)  41.9 us
    unnamed x3, other arithmetic  29 us
  transfers between devices with their start and end apart: 7, of which 5 were waited for; matrix products, arithmetic and copies ran while one was open for 22% of the time, Pallas kernels for 0%

commit v1 on v0

--- a/solution.py
+++ b/solution.py
@@ -4,6 +4,18 @@
 from jax.sharding import PartitionSpec as P
 
 TSTEPS = 3
+
+
+def cut_along(shard, dim, size):
+    lengths = shard.shape
+    blocks = shard.reshape(*lengths[:dim], size, lengths[dim] // size, *lengths[dim + 1 :])
+    return jnp.moveaxis(blocks, dim, 0)
+
+
+def joined_along(blocks, dim):
+    shape = list(blocks.shape[1:])
+    shape[dim] *= blocks.shape[0]
+    return jnp.moveaxis(blocks, 0, dim).reshape(shape)
 
 
 def shards(weight, leak, rates, cotangent):
@@ -18,7 +30,14 @@
         scaled = leak[None, :] * carried
         spread = scaled.reshape(own_rows, local_units // n_col, n_col)
         by_col = lax.all_to_all(spread, "col", split_axis=2, concat_axis=1, tiled=True)
-        by_row = lax.all_to_all(by_col, "row", split_axis=1, concat_axis=0, tiled=True)
+        size, index = (lax.axis_size("row"), lax.axis_index("row"))
+        parts = cut_along(by_col, 1, size)
+        outs = [parts[index]]
+        for step in range(1, size):
+            sent = parts[index ^ step]
+            outs.append(lax.ppermute(sent, "row", [(i, i ^ step) for i in range(size)]))
+        parts = jnp.stack(outs)[index ^ jnp.arange(size)]
+        by_row = joined_along(parts, 0)
         gathered = lax.all_gather(by_row, "col", axis=2, tiled=True)
         unit_block = gathered.reshape(gathered.shape[0], gathered.shape[1] * gathered.shape[2])
         rates_now = full_rates[step_back]

time: 642 us -> 613 us (0.955)
  blocking collectives: 109 us -> 26.5 us
  waiting for transfers between devices: 213 us -> 288 us
  other arithmetic: 50.4 us -> 15.1 us
  starting transfers between devices: 1 us -> 19.1 us
    all_to_all x3 -> x0, blocking collectives: 67.2 us -> none  [shards(): lax.all_to_all(by_col, 'row', split_axis=1, concat_axis=0, tiled=True)]
    ppermute x0 -> x9, waiting for transfers between devices: none -> 33 us  [shards(): outs.append(lax.ppermute(sent, 'row', [(i, i ^ step) for i in range(size)]))]
    unnamed x3 -> x0, other arithmetic: 29 us -> none
    all_gather x1, waiting for transfers between devices: 57.2 us -> 84.4 us  [shards(): full_rates = lax.all_gather(rates, 'row', axis=1, tiled=True)]
    all_to_all x3 -> x2, blocking collectives: 41.9 us -> 26.5 us  [shards(): lax.all_to_all(spread, 'col', split_axis=2, concat_axis=1, tiled=True)]
    ppermute x0 -> x9, starting transfers between devices: none -> 13.4 us  [shards(): outs.append(lax.ppermute(sent, 'row', [(i, i ^ step) for i in range(size)]))]
    all_to_all x0 -> x1, waiting for transfers between devices: none -> 9.65 us  [shards(): lax.all_to_all(spread, 'col', split_axis=2, concat_axis=1, tiled=True)]
    unnamed x17 -> x22, local copies, waits for them, and re-layouts: 7.58 us -> 0.14 us
  transfers between devices with their start and end apart: 7 -> 17, of which waited for: 5 -> 13; matrix products, arithmetic and copies ran while one was open for 22% -> 20% of each run, Pallas kernels for 0% -> 0%
where the time goes in v1:
time: 613 us; the launch traced here: 604 us
  waiting for transfers between devices  288 us (47%)
  matrix products  213 us (35%)
  local copies, waits for them, and re-layouts  27.5 us (4%)
  blocking collectives  26.5 us (4%)
  starting transfers between devices  19.1 us (3%)
  other arithmetic  15.1 us (2%)
  between operations  14.6 us (2%)
    dot_general x3, matrix products, shards(): lax.dot_general(unit_block, rates_now, (((0,), (0,)), ((), ())), precisio...  111 us
    dot_general x3, matrix products, shards(): jnp.dot(unit_block, weight, precision=lax.Precision.HIGHEST, preferred_el...  102 us
    reduce_scatter x3, waiting for transfers between devices, shards(): lax.psum_scatter(partial_sum, 'row', scatter_dimension=0, tiled=True)  86.9 us
    all_gather x1, waiting for transfers between devices, shards(): full_rates = lax.all_gather(rates, 'row', axis=1, tiled=True)  84.4 us
    all_gather x3, waiting for transfers between devices, shards(): gathered = lax.all_gather(by_row, 'col', axis=2, tiled=True)  73.9 us
    ppermute x9, waiting for transfers between devices, shards(): outs.append(lax.ppermute(sent, 'row', [(i, i ^ step) for i in range(size)]))  33 us
    all_to_all x2, blocking collectives, shards(): lax.all_to_all(spread, 'col', split_axis=2, concat_axis=1, tiled=True)  26.5 us
    all_gather x3, local copies, waits for them, and re-layouts, shards(): gathered = lax.all_gather(by_row, 'col', axis=2, tiled=True)  16.4 us
  transfers between devices with their start and end apart: 17, of which 13 were waited for; matrix products, arithmetic and copies ran while one was open for 20% of the time, Pallas kernels for 0%

profile of v1, /device:TPU:0, one launch (start us, length us, event | category | flops | bytes accessed | tf_op | source)
XLA Modules:
  0.0 604.4 jit_solution(4690669527978263931)
XLA Ops:
  7.2 1.1 broadcast_multiply_fusion.2
  8.3 0.3 copy.28
  8.6 1.2 copy.29
  9.8 5.2 all-to-all-start
  15.0 9.6 %all-to-all-done = f32[64,256,8]{1,0,2:T(8,128)S(1)} async-done(((f32[64,256,8]{1,0,2:T(8,128)}), f32[64,256,8]{1,0,2:T(8,128)S(1)}, u32[]{:S(2)}, u32[]{:S(2)}) %all-to-all-start) | async-done | bytes 524320 | tf_op jit(solution)/shard_map/all_to_all | solution.py:32
  24.7 0.3 copy.30
  25.0 0.2 reshape.101
  25.2 0.5 constant_dynamic-slice_fusion.11
  25.8 1.6 collective-permute-start
  27.4 2.6 collective-permute-start.1
  30.0 0.2 collective-permute-start.2
  30.3 1.0 collective-permute-done
  31.3 6.7 %collective-permute-done.1 = f32[64,512,1]{1,0,2:T(8,128)S(1)} collective-permute-done((f32[64,512,1]{1,0,2:T(8,128)S(1)}, f32[64,512,1]{1,0,2:T(8,128)S(1)}, u32[]{:S(2)}, u32[]{:S(2)}) %collective-permute-start.1) | collective-permute-done | bytes 131104 | tf_op jit(solution)/shard_map/ppermute | solution.py:38
  38.1 1.4 gather_fusion
  39.5 38.0 %all-gather.5.cloned.1.call-done = f32[256,512,8]{1,0,2:T(8,128)} async-done(((f32[256,512,1]{1,0,2:T(8,128)}), f32[256,512,8]{1,0,2:T(8,128)}) %all-gather.5.cloned.1.call-update) | async-done | bytes 4194320 | tf_op jit(solution)/shard_map/all_gather | solution.py:41
  77.5 5.5 copy.31
  83.0 33.8 %fusion.9 = f32[256,2048]{1,0:T(8,128)} fusion(f32[4096,2048]{1,0:T(8,128)} %param.4, f32[256,512,8]{0,2,1:T(8,128)} %copy.31), kind=kOutput, calls=%fused_computation.13 | convolution fusion | flops 25769803776 | bytes 39845888 | tf_op jit(solution)/shard_map/dot_general | solution.py:52
  116.9 43.7 %reduce-scatter.4.cloned.1.call-done = f32[64,2048]{1,0:T(8,128)} async-done(((f32[256,2048]{1,0:T(8,128)}), f32[64,2048]{1,0:T(8,128)}) %reduce-scatter.4.cloned.1.call-update) | async-done | bytes 524304 | tf_op jit(solution)/shard_map/reduce_scatter | solution.py:55
  160.7 1.3 broadcast_multiply_fusion.1
  162.0 0.3 copy.32
  162.3 0.4 copy.33
  162.7 13.4 %all_to_all.45 = f32[64,256,8]{1,0,2:T(8,128)S(1)} all-to-all(f32[64,256,8]{1,0,2:T(8,128)S(1)} %copy.33), channel_id=1, replica_groups=mesh['row'=4,'col'=8] {'col'}, dimensions={2} | all-to-all | bytes 1048576 | tf_op jit(solution)/shard_map/all_to_all | solution.py:32
  176.0 0.3 copy.34
  176.4 0.2 reshape.105
  176.6 0.5 constant_dynamic-slice_fusion.7
  177.1 0.7 collective-permute-start.3
  177.8 1.5 collective-permute-start.4
  179.3 2.3 collective-permute-start.5
  181.6 2.0 collective-permute-done.3
  183.6 6.6 %collective-permute-done.4 = f32[64,512,1]{1,0,2:T(8,128)S(1)} collective-permute-done((f32[64,512,1]{1,0,2:T(8,128)S(1)}, f32[64,512,1]{1,0,2:T(8,128)S(1)}, u32[]{:S(2)}, u32[]{:S(2)}) %collective-permute-start.4) | collective-permute-done | bytes 131104 | tf_op jit(solution)/shard_map/ppermute | solution.py:38
  190.2 1.4 gather_fusion.1
  191.7 36.0 %all-gather.7.cloned.1.call-done = f32[256,512,8]{1,0,2:T(8,128)} async-done(((f32[256,512,1]{1,0,2:T(8,128)}), f32[256,512,8]{1,0,2:T(8,128)}) %all-gather.7.cloned.1.call-update) | async-done | bytes 4194320 | tf_op jit(solution)/shard_map/all_gather | solution.py:41
  227.6 5.5 copy.35
  233.1 33.8 %fusion.5 = f32[256,2048]{1,0:T(8,128)} fusion(f32[4096,2048]{1,0:T(8,128)} %param.4, f32[256,512,8]{0,2,1:T(8,128)} %copy.35), kind=kOutput, calls=%fused_computation.9 | convolution fusion | flops 25769803776 | bytes 39845888 | tf_op jit(solution)/shard_map/dot_general | solution.py:52
  267.0 0.5 all-gather.11.cloned.1.call-update
  267.6 43.2 %reduce-scatter.6.cloned.1.call-done = f32[64,2048]{1,0:T(8,128)} async-done(((f32[256,2048]{1,0:T(8,128)}), f32[64,2048]{1,0:T(8,128)}) %reduce-scatter.6.cloned.1.call-update) | async-done | bytes 524304 | tf_op jit(solution)/shard_map/reduce_scatter | solution.py:55
  310.8 2.0 broadcast_multiply_fusion
  312.8 0.3 copy.36
  313.2 0.4 copy.37
  313.5 13.2 %all_to_all.46 = f32[64,256,8]{1,0,2:T(8,128)S(1)} all-to-all(f32[64,256,8]{1,0,2:T(8,128)S(1)} %copy.37), channel_id=1, replica_groups=mesh['row'=4,'col'=8] {'col'}, dimensions={2} | all-to-all | bytes 1048576 | tf_op jit(solution)/shard_map/all_to_all | solution.py:32
  326.7 0.3 copy.38
  327.0 0.2 reshape.109
  327.3 0.5 constant_dynamic-slice_fusion.3
  327.8 0.7 collective-permute-start.6
  328.5 1.5 collective-permute-start.7
  330.0 2.3 collective-permute-start.8
  332.3 9.6 %collective-permute-done.6 = f32[64,512,1]{1,0,2:T(8,128)S(1)} collective-permute-done((f32[64,512,1]{1,0,2:T(8,128)S(1)}, f32[64,512,1]{1,0,2:T(8,128)S(1)}, u32[]{:S(2)}, u32[]{:S(2)}) %collective-permute-start.6) | collective-permute-done | bytes 131104 | tf_op jit(solution)/shard_map/ppermute | solution.py:38
  341.9 6.3 %collective-permute-done.7 = f32[64,512,1]{1,0,2:T(8,128)S(1)} collective-permute-done((f32[64,512,1]{1,0,2:T(8,128)S(1)}, f32[64,512,1]{1,0,2:T(8,128)S(1)}, u32[]{:S(2)}, u32[]{:S(2)}) %collective-permute-start.7) | collective-permute-done | bytes 131104 | tf_op jit(solution)/shard_map/ppermute | solution.py:38
  348.2 0.7 collective-permute-done.8
  348.9 1.4 gather_fusion.2
  350.3 0.3 reduce-scatter.8.cloned.1.call-start
  350.5 2.6 reduce_sum.29
  353.3 0.2 stack.62
  353.5 84.4 %all-gather.11.cloned.1.call-done = f32[3,256,2048]{2,1,0:T(8,128)} async-done(((f32[3,64,2048]{2,1,0:T(8,128)}), f32[3,256,2048]{2,1,0:T(8,128)}) %all-gather.11.cloned.1.call-update) | async-done | bytes 6291472 | tf_op jit(solution)/shard_map/all_gather | solution.py:25
  437.9 32.4 %fusion.7 = f32[4096,2048]{1,0:T(8,128)} fusion(f32[256,512,8]{0,2,1:T(8,128)} %copy.31, f32[3,256,2048]{2,1,0:T(8,128)} %all-gather.11.cloned.1.call-done), kind=kOutput, calls=%fused_computation.11 | convolution fusion | flops 25769803776 | bytes 39845888 | tf_op jit(solution)/shard_map/dot_general | solution.py:45
  470.2 2.7 reduce_sum.28
  473.0 0.2 stack.61
  473.2 32.5 %fusion.3 = f32[4096,2048]{1,0:T(8,128)} fusion(f32[256,512,8]{0,2,1:T(8,128)} %copy.35, f32[3,256,2048]{2,1,0:T(8,128)} %all-gather.11.cloned.1.call-done), kind=kOutput, calls=%fused_computation.7 | convolution fusion | flops 25769803776 | bytes 39845888 | tf_op jit(solution)/shard_map/dot_general | solution.py:45
  505.7 2.6 reduce_sum.27
  508.6 5.5 copy.39
  514.1 34.2 %fusion.1 = f32[256,2048]{1,0:T(8,128)} fusion(f32[4096,2048]{1,0:T(8,128)} %param.4, f32[256,512,8]{0,2,1:T(8,128)} %copy.39), kind=kOutput, calls=%fused_computation.5 | convolution fusion | flops 25769803776 | bytes 39845888 | tf_op jit(solution)/shard_map/dot_general | solution.py:52
  548.4 0.7 pad_maximum_fusion
  549.0 46.4 %add_add_fusion = f32[4096,2048]{1,0:T(8,128)} fusion(f32[4096,2048]{1,0:T(8,128)} %fusion.7, f32[4096,2048]{1,0:T(8,128)} %fusion.3, f32[256,512,8]{0,2,1:T(8,128)} %copy.39, f32[3,256,2048]{2,1,0:T(8,128)} %all-gather.11.cloned.1.call-done), kind=kOutput, calls=%fused_computation.3 | convolution fusion | flops 25786580992 | bytes 106954752 | tf_op jit(solution)/shard_map/dot_general | solution.py:45
  595.4 1.9 fusion.11
  (48 shorter events, 1.1 us)
Async XLA Ops:
  9.8 14.9 %all-to-all-start = ((f32[64,256,8]{1,0,2:T(8,128)}), f32[64,256,8]{1,0,2:T(8,128)S(1)}, u32[]{:S(2)}, u32[]{:S(2)}) async-start(f32[64,256,8]{1,0,2:T(8,128)} %copy.29), calls=%async_computation | async-start | bytes 1048576 | tf_op jit(solution)/shard_map/all_to_all | solution.py:32
  15.0 62.5 %all-gather.5.cloned.1.call-start = ((), (), s32[]{:S(2)}) async-start(), calls=%async_computation.6 | async-start | bytes 4718592 | tf_op jit(solution)/shard_map/all_gather | solution.py:41
  25.8 5.5 collective-permute-start
  27.4 10.6 %collective-permute-start.1 = (f32[64,512,1]{1,0,2:T(8,128)S(1)}, f32[64,512,1]{1,0,2:T(8,128)S(1)}, u32[]{:S(2)}, u32[]{:S(2)}) collective-permute-start(f32[64,512,1]{1,0,2:T(8,128)S(1)} %bitcast.140), channel_id=1, source_target_pairs={{0,16},{8,24},{16,0},{24,8},{1,17},{9,25},{17,1},{25,9},{2,18},{10... | collective-permute-start | bytes 393224 | tf_op jit(solution)/shard_map/ppermute | solution.py:38
  30.0 8.0 %collective-permute-start.2 = (f32[64,512,1]{1,0,2:T(8,128)S(1)}, f32[64,512,1]{1,0,2:T(8,128)S(1)}, u32[]{:S(2)}, u32[]{:S(2)}) collective-permute-start(f32[64,512,1]{1,0,2:T(8,128)S(1)} %bitcast.137), channel_id=1, source_target_pairs={{0,24},{8,16},{16,8},{24,0},{1,25},{9,17},{17,9},{25,1},{2,26},{10... | collective-permute-start | bytes 393224 | tf_op jit(solution)/shard_map/ppermute | solution.py:38
  39.5 121.2 %reduce-scatter.4.cloned.1.call-start = ((), (), s32[]{:S(2)}) async-start(), calls=%async_computation.7 | async-start | bytes 2621440 | tf_op jit(solution)/shard_map/reduce_scatter | solution.py:55
  83.0 33.9 %copy-start.4 = (f32[2048]{0:T(1024)S(1)}, f32[2048]{0:T(1024)}, u32[]{:S(2)}) copy-start(f32[2048]{0:T(1024)} %param.5) | copy-start | bytes 24580
  83.0 77.7 %copy-start.1 = (f32[64,2048]{1,0:T(8,128)S(1)}, f32[64,2048]{1,0:T(8,128)}, u32[]{:S(2)}) copy-start(f32[64,2048]{1,0:T(8,128)} %param.7) | copy-start | bytes 1572868
  116.9 110.8 %all-gather.7.cloned.1.call-start = ((), (), s32[]{:S(2)}) async-start(), calls=%async_computation.8 | async-start | bytes 4718592 | tf_op jit(solution)/shard_map/all_gather | solution.py:41
  177.1 6.4 %collective-permute-start.3 = (f32[64,512,1]{1,0,2:T(8,128)S(1)}, f32[64,512,1]{1,0,2:T(8,128)S(1)}, u32[]{:S(2)}, u32[]{:S(2)}) collective-permute-start(f32[64,512,1]{1,0,2:T(8,128)S(1)} %bitcast.144), channel_id=1, source_target_pairs={{0,8},{8,0},{16,24},{24,16},{1,9},{9,1},{17,25},{25,17},{2,10},{10... | collective-permute-start | bytes 393224 | tf_op jit(solution)/shard_map/ppermute | solution.py:38
  177.8 12.3 %collective-permute-start.4 = (f32[64,512,1]{1,0,2:T(8,128)S(1)}, f32[64,512,1]{1,0,2:T(8,128)S(1)}, u32[]{:S(2)}, u32[]{:S(2)}) collective-permute-start(f32[64,512,1]{1,0,2:T(8,128)S(1)} %bitcast.141), channel_id=1, source_target_pairs={{0,16},{8,24},{16,0},{24,8},{1,17},{9,25},{17,1},{25,9},{2,18},{10... | collective-permute-start | bytes 393224 | tf_op jit(solution)/shard_map/ppermute | solution.py:38
  179.3 10.9 %collective-permute-start.5 = (f32[64,512,1]{1,0,2:T(8,128)S(1)}, f32[64,512,1]{1,0,2:T(8,128)S(1)}, u32[]{:S(2)}, u32[]{:S(2)}) collective-permute-start(f32[64,512,1]{1,0,2:T(8,128)S(1)} %bitcast.138), channel_id=1, source_target_pairs={{0,24},{8,16},{16,8},{24,0},{1,25},{9,17},{17,9},{25,1},{2,26},{10... | collective-permute-start | bytes 393224 | tf_op jit(solution)/shard_map/ppermute | solution.py:38
  191.6 119.1 %reduce-scatter.6.cloned.1.call-start = ((), (), s32[]{:S(2)}) async-start(), calls=%async_computation.9 | async-start | bytes 2621440 | tf_op jit(solution)/shard_map/reduce_scatter | solution.py:55
  233.1 77.7 %copy-start.3 = (f32[64,2048]{1,0:T(8,128)S(1)}, f32[64,2048]{1,0:T(8,128)}, u32[]{:S(2)}) copy-start(f32[64,2048]{1,0:T(8,128)} %reduce-scatter.4.cloned.1.call-done) | copy-start | bytes 1572868
  267.0 43.8 %copy-start = (f32[3,64,2048]{2,1,0:T(8,128)S(1)}, f32[3,64,2048]{2,1,0:T(8,128)}, u32[]{:S(2)}) copy-start(f32[3,64,2048]{2,1,0:T(8,128)} %param.6) | copy-start | bytes 4718596
  267.0 170.9 %all-gather.11.cloned.1.call-start = ((), (), s32[]{:S(2)}) async-start(), calls=%async_computation.12 | async-start | bytes 7864320 | tf_op jit(solution)/shard_map/all_gather | solution.py:25
  267.6 238.1 %all-gather.9.cloned.1.call-start = ((), (), s32[]{:S(2)}) async-start(), calls=%async_computation.10 | async-start | bytes 4718592 | tf_op jit(solution)/shard_map/all_gather | solution.py:41
  327.8 14.1 %collective-permute-start.6 = (f32[64,512,1]{1,0,2:T(8,128)S(1)}, f32[64,512,1]{1,0,2:T(8,128)S(1)}, u32[]{:S(2)}, u32[]{:S(2)}) collective-permute-start(f32[64,512,1]{1,0,2:T(8,128)S(1)} %bitcast.145), channel_id=1, source_target_pairs={{0,8},{8,0},{16,24},{24,16},{1,9},{9,1},{17,25},{25,17},{2,10},{10... | collective-permute-start | bytes 393224 | tf_op jit(solution)/shard_map/ppermute | solution.py:38
  328.5 19.7 %collective-permute-start.7 = (f32[64,512,1]{1,0,2:T(8,128)S(1)}, f32[64,512,1]{1,0,2:T(8,128)S(1)}, u32[]{:S(2)}, u32[]{:S(2)}) collective-permute-start(f32[64,512,1]{1,0,2:T(8,128)S(1)} %bitcast.142), channel_id=1, source_target_pairs={{0,16},{8,24},{16,0},{24,8},{1,17},{9,25},{17,1},{25,9},{2,18},{10... | collective-permute-start | bytes 393224 | tf_op jit(solution)/shard_map/ppermute | solution.py:38
  330.0 18.9 %collective-permute-start.8 = (f32[64,512,1]{1,0,2:T(8,128)S(1)}, f32[64,512,1]{1,0,2:T(8,128)S(1)}, u32[]{:S(2)}, u32[]{:S(2)}) collective-permute-start(f32[64,512,1]{1,0,2:T(8,128)S(1)} %bitcast.139), channel_id=1, source_target_pairs={{0,24},{8,16},{16,8},{24,0},{1,25},{9,17},{17,9},{25,1},{2,26},{10... | collective-permute-start | bytes 393224 | tf_op jit(solution)/shard_map/ppermute | solution.py:38
  350.3 245.1 %reduce-scatter.8.cloned.1.call-start = ((), (), s32[]{:S(2)}) async-start(), calls=%async_computation.11 | async-start | bytes 2621440 | tf_op jit(solution)/shard_map/reduce_scatter | solution.py:55
  549.0 46.4 %copy-start.2 = (f32[64,2048]{1,0:T(8,128)S(1)}, f32[64,2048]{1,0:T(8,128)}, u32[]{:S(2)}) copy-start(f32[64,2048]{1,0:T(8,128)} %get-tuple-element.4) | copy-start | bytes 1572868
Sparse Core Ops, SparseCore 0:
  39.6 37.8 all-gather.4
  117.0 43.6 reduce-scatter.3
  191.7 35.8 all-gather.6
  267.1 43.6 reduce-scatter.5
  312.2 125.6 all-gather.10
  439.6 34.7 all-gather.8
  548.5 41.7 reduce-scatter.7
